TPU v7x, 32 devices: a whole 2x2x4 slice. The times are simulated.
32 devices in a mesh: facet: 8 (over z, x), strip: 4 (over y, core).
Axes of the slice: x: 2, y: 2, z: 4, core: 2. Of those that a mesh axis runs over, the one named last changes fastest.
Arguments:
- facets: bfloat16 [8, 2, 512, 8192], P('facet', None, None, 'strip'), may hold values from -6 to 6
- offsets: int32 [4], replicated, may hold values from 0 to 32767
- visibilities: float32 [2, 512, 2048], P(None, 'strip', 'facet'), may hold values from -24 to 24
- weights: float32 [512, 2048], P('strip', 'facet'), may hold values from 0.1 to 1
- mask: int32 [512, 2048], P('strip', 'facet'), may hold values 0 or 1
Outputs:
- facet_update: bfloat16 [8, 2, 512, 8192], P('facet', None, None, 'strip')
Inputs may be any that keep to these rules, and one draw needn't show every extreme that they name: `mask`: 1 where the cell holds a sampled visibility.
All inputs are finite; a program needn't handle non-finite values. No bound on the sum of `mask` on one device may be relied on, other than what follows from the above.
Results may differ from a plain program's by a relative error of at most 0.0058.
Values may be sent and summed in bfloat16 or wider, within the bound.
No kernel may reach another device: no remote copies, remote signals or barrier semaphores. Data moves between devices by JAX's collectives and lax.ppermute only.
A program may use at most 128 MiB of HBM per device.

v0:
```python
import math
import jax
import jax.numpy as jnp
from jax import lax
from jax.sharding import PartitionSpec as P

NG = 32768
XM = 8192
SG = 512
NSUB = 4
FROWS = 4


def residue_angle(count):
    return count.astype(jnp.float32) * (2.0 * math.pi / NG)


def dft_kernel(rows):
    positions = jnp.arange(rows, dtype=jnp.int32)
    cells = jnp.arange(SG, dtype=jnp.int32)
    angle = residue_angle(positions[:, None] * cells[None, :] % NG)
    return jnp.concatenate([jnp.cos(angle), jnp.sin(angle)], axis=1).astype(jnp.bfloat16)


def row_angles(start, rows, offsets):
    positions = start + jnp.arange(rows, dtype=jnp.int32)
    return residue_angle(offsets[:, None] * positions[None, :] % NG)


def column_angles(facet_index, offsets):
    centre = (facet_index % FROWS * XM + NG // 2) % NG
    cells = jnp.arange(SG, dtype=jnp.int32)
    return residue_angle((cells[None, :] * centre % NG + offsets[:, None] * centre % NG) % NG)


def forward(data, start, facet_index, offsets, kernel_table):
    columns = data.shape[1]
    rows = data.shape[2]
    phi = row_angles(start, rows, offsets)[:, None, :]
    cos_phi = jnp.cos(phi)
    sin_phi = jnp.sin(phi)
    real_part = data[0].astype(jnp.float32)[None]
    imag_part = data[1].astype(jnp.float32)[None]
    twisted = jnp.stack(
        [real_part * cos_phi + imag_part * sin_phi, imag_part * cos_phi - real_part * sin_phi],
        axis=1,
    ).astype(jnp.bfloat16)
    spectra = jnp.dot(twisted.reshape(-1, rows), kernel_table, preferred_element_type=jnp.float32)
    spectra = spectra.reshape(NSUB, 2, columns, 2, SG)
    spectrum_real = spectra[:, 0, :, 0] + spectra[:, 1, :, 1]
    spectrum_imag = spectra[:, 1, :, 0] - spectra[:, 0, :, 1]
    psi = column_angles(facet_index, offsets)[:, None, :]
    cos_psi = jnp.cos(psi)
    sin_psi = jnp.sin(psi)
    scale = 1.0 / math.sqrt(XM)
    result_real = (spectrum_real * cos_psi + spectrum_imag * sin_psi) * scale
    result_imag = (spectrum_imag * cos_psi - spectrum_real * sin_psi) * scale
    stacked = jnp.stack([result_real, result_imag])
    return stacked.transpose(0, 2, 1, 3).reshape(2, columns, NSUB * SG)


def adjoint(residual, start, facet_index, offsets, kernel_table):
    columns = residual.shape[1]
    rows = kernel_table.shape[0]
    values = residual.astype(jnp.float32).reshape(2, columns, NSUB, SG).transpose(0, 2, 1, 3)
    psi = column_angles(facet_index, offsets)[:, None, :]
    cos_psi = jnp.cos(psi)
    sin_psi = jnp.sin(psi)
    first = values[0] * cos_psi - values[1] * sin_psi
    second = values[1] * cos_psi + values[0] * sin_psi
    untwisted = jnp.stack([first, second], axis=1).astype(jnp.bfloat16)
    images = jnp.einsum(
        "mj,xpj->pmx",
        untwisted.reshape(-1, SG),
        kernel_table.reshape(rows, 2, SG),
        preferred_element_type=jnp.float32,
    )
    images = images.reshape(2, NSUB, 2, columns, rows)
    image_real = images[0, :, 0] - images[1, :, 1]
    image_imag = images[0, :, 1] + images[1, :, 0]
    phi = row_angles(start, rows, offsets)[:, None, :]
    cos_phi = jnp.cos(phi)
    sin_phi = jnp.sin(phi)
    scale = 1.0 / math.sqrt(XM)
    total_real = jnp.sum(image_real * cos_phi - image_imag * sin_phi, axis=0) * scale
    total_imag = jnp.sum(image_imag * cos_phi + image_real * sin_phi, axis=0) * scale
    return jnp.stack([total_real, total_imag])


def weigh(model, visibilities, weights, mask):
    factor = weights * mask.astype(jnp.float32)
    return (factor[None] * (visibilities - model)).astype(jnp.bfloat16)


def on_device(facets, offsets, visibilities, weights, mask):
    facet_index = lax.axis_index("facet")
    regrouped = lax.all_to_all(facets[0], "strip", split_axis=1, concat_axis=2, tiled=True)
    kernel_table = dft_kernel(regrouped.shape[2])
    contribution = forward(regrouped, 0, facet_index, offsets, kernel_table)
    model = lax.psum_scatter(contribution, "facet", scatter_dimension=2, tiled=True)
    residual = weigh(model, visibilities, weights, mask)
    gathered = lax.all_gather(residual, "facet", axis=2, tiled=True)
    update = adjoint(gathered, 0, facet_index, offsets, kernel_table).astype(jnp.bfloat16)
    result = lax.all_to_all(update, "strip", split_axis=2, concat_axis=1, tiled=True)
    return result[None]


def solution(mesh):
    placed = (
        P("facet", None, None, "strip"),
        P(),
        P(None, "strip", "facet"),
        P("strip", "facet"),
        P("strip", "facet"),
    )
    return jax.shard_map(
        on_device,
        mesh=mesh,
        in_specs=placed,
        out_specs=P("facet", None, None, "strip"),
        check_vma=False,
    )
```

profile of v0, /device:TPU:0, one launch (start us, length us, event | category | flops | bytes accessed | tf_op | source)
XLA Modules:
  0.0 451.6 jit_solution(7619882456607674424)
XLA Ops:
  6.5 8.5 %copy.105 = bf16[1,2,512,2048]{3,1,2,0:T(2,128)(2,1)} copy(bf16[1,2,512,2048]{3,2,1,0:T(8,128)(2,1)} %param.5) | data formatting | bytes 8388608 | tf_op args[0]
  15.1 4.9 %all-to-all-start = ((bf16[2,512,2048]{2,0,1:T(2,128)(2,1)}), bf16[2,512,2048]{2,0,1:T(2,128)(2,1)}, u32[]{:S(2)}, u32[]{:S(2)}) async-start(bf16[2,512,2048]{2,0,1:T(2,128)(2,1)} %bitcast.137), calls=%async_computation | async-start | bytes 8388608 | tf_op jit(solution)/shard_map/all_to_all | solution.py:97
  19.9 0.2 reduce-scatter.2.cloned.1.call-start
  20.2 67.2 %sine_convert_fusion = (bf16[8192,512]{0,1:T(8,128)(2,1)}, bf16[8192,512]{0,1:T(8,128)(2,1)}) fusion(), kind=kLoop, calls=%fused_computation.31 | loop fusion | flops 67108864 | bytes 16777216 | tf_op jit(solution)/shard_map/convert.11
  87.6 13.7 %pad_maximum_fusion = bf16[8192,1024]{0,1:T(8,128)(2,1)} fusion(bf16[8192,512]{0,1:T(8,128)(2,1)} %get-tuple-element.19, bf16[8192,512]{0,1:T(8,128)(2,1)} %get-tuple-element.20), kind=kLoop, calls=%fused_computation.28 | loop fusion | flops 33554432 | bytes 33554432 | tf_op jit(solution)/shard_map/concatenate | solution.py:22
  101.3 1.2 fusion.32
  102.5 4.1 copy.77
  106.6 4.4 slice_convert_fusion.1
  111.0 5.3 %copy.78 = f32[1,128,4,2048]{1,3,2,0:T(8,128)} copy(f32[1,128,4,2048]{3,1,2,0:T(8,128)} %get-tuple-element.11) | data formatting | bytes 8388608 | tf_op jit(solution)/shard_map/convert_element_type | solution.py:42
  116.3 5.6 %copy.79 = f32[128,8192]{1,0:T(8,128)} copy(f32[128,8192]{0,1:T(8,128)} %bitcast.138) | data formatting | bytes 8388608 | tf_op jit(solution)/shard_map/convert_element_type | solution.py:42
  121.9 5.3 %copy.80 = f32[1,128,4,2048]{1,3,2,0:T(8,128)} copy(f32[1,128,4,2048]{3,1,2,0:T(8,128)} %get-tuple-element.12) | data formatting | bytes 8388608 | tf_op jit(solution)/shard_map/convert_element_type | solution.py:43
  127.3 5.6 %copy.81 = f32[128,8192]{1,0:T(8,128)} copy(f32[128,8192]{0,1:T(8,128)} %bitcast.139) | data formatting | bytes 8388608 | tf_op jit(solution)/shard_map/convert_element_type | solution.py:43
  132.9 6.5 %add_convert_fusion = (bf16[4,1,128,8192]{3,2,1,0:T(8,128)(2,1)S(1)}, bf16[4,1,128,8192]{3,2,1,0:T(8,128)(2,1)S(1)}) fusion(f32[4,8192]{1,0:T(4,128)S(1)} %get-tuple-element.18, f32[128,8192]{1,0:T(8,128)} %copy.81, f32[4,8192]{1,0:T(4,128)S(1)} %get-tuple-element.17, f32[128,8192]{1,0:T(8,128)} %copy.79), kind=kLoop, calls=%fused_computation.36 | loop fusion | flops 33554432 | bytes 25427968 | tf_op jit(solution)/shard_map/convert.12
  139.4 21.8 %fusion.14 = f32[4,2,128,2,512]{4,2,3,1,0:T(8,128)S(1)} fusion(bf16[2,512,8192,1,1]{2,1,0,4,3:T(8,128)(2,1)} %bitcast.136, bf16[4,1,128,8192]{3,2,1,0:T(8,128)(2,1)S(1)} %get-tuple-element.8, bf16[4,1,128,8192]{3,2,1,0:T(8,128)(2,1)S(1)} %get-tuple-element.7), kind=kOutput, calls=%fused_computation.25 | convolution fusion | flops 17213423616 | bytes 37748736 | tf_op jit(solution)/shard_map/dot_general | solution.py:48
  161.2 0.7 add_multiply_fusion
  161.9 0.2 maximum_bitcast_fusion.2
  162.1 1.8 copy.84
  164.0 0.3 all-gather.2.cloned.1.call-start
  164.5 70.9 %reduce-scatter.2.cloned.1.call-done = f32[2,128,256]{1,2,0:T(8,128)} async-done(((f32[2,128,2048]{1,2,0:T(8,128)}), f32[2,128,256]{1,2,0:T(8,128)}) %reduce-scatter.2.cloned.1.call-update) | async-done | bytes 262160 | tf_op jit(solution)/shard_map/reduce_scatter | solution.py:100
  235.4 1.6 multiply_convert_fusion.2
  237.0 68.4 %sine_convert_fusion.1 = (bf16[8192,1,512]{2,0,1:T(8,128)(2,1)}, bf16[8192,1,512]{2,0,1:T(8,128)(2,1)}) fusion(), kind=kLoop, calls=%fused_computation.37 | loop fusion | flops 67108864 | bytes 16777216 | tf_op jit(solution)/shard_map/convert.15
  305.4 1.5 copy.86
  306.9 0.3 subtract_convert_fusion.1
  307.3 31.5 %fusion.10 = f32[8192,2,1024]{0,2,1:T(8,128)} fusion(bf16[1024,512,1]{1,0,2:T(8,128)(2,1)S(1)} %bitcast.144, bf16[8192,1,512]{2,0,1:T(8,128)(2,1)} %get-tuple-element.21, bf16[8192,1,512]{2,0,1:T(8,128)(2,1)} %get-tuple-element.22), kind=kOutput, calls=%fused_computation.20 | convolution fusion | flops 17188257792 | bytes 84934656 | tf_op jit(solution)/shard_map/mj,xpj->pmx/dot_general | solution.py:72
  338.8 26.7 %subtract_reduce_fusion = (f32[128,8192]{1,0:T(8,128)}, f32[128,8192]{1,0:T(8,128)}) fusion(f32[4,8192]{1,0:T(4,128)S(1)} %get-tuple-element.18, f32[4,8192]{1,0:T(4,128)S(1)} %get-tuple-element.17, f32[2,4,2,128,8192]{4,3,2,1,0:T(8,128)} %bitcast.25), kind=kLoop, calls=%fused_computation.30 | loop fusion | flops 39845888 | bytes 75759616 | tf_op jit(solution)/shard_map/reduce_sum | solution.py:85
  365.5 2.6 fusion.23
  368.0 2.6 fusion.24
  370.6 2.4 pad_maximum_fusion.1
  373.0 11.1 %copy.93 = bf16[2,128,8192]{1,0,2:T(2,128)(2,1)} copy(bf16[2,128,8192]{2,1,0:T(8,128)(2,1)} %pad_maximum_fusion.1) | data formatting | bytes 8388608 | tf_op jit(solution)/shard_map/stack | solution.py:87
  384.1 51.9 %all_to_all.30 = bf16[2,128,8192]{1,0,2:T(2,128)(2,1)S(1)} all-to-all(bf16[2,128,8192]{1,0,2:T(2,128)(2,1)} %copy.93), channel_id=1, replica_groups=mesh['facet'=8,'strip'=4] {'strip'}, dimensions={2} | all-to-all | bytes 8388608 | tf_op jit(solution)/shard_map/all_to_all | solution.py:104
  436.0 2.5 copy.94
  438.5 6.2 %copy.95 = bf16[2,4,128,2048]{3,2,1,0:T(8,128)(2,1)} copy(bf16[2,4,128,2048]{2,3,1,0:T(8,128)(2,1)} %bitcast.140) | data formatting | bytes 8388608 | tf_op jit(solution)/shard_map/all_to_all | solution.py:104
  (19 shorter events, 0.6 us)
Async XLA Ops:
  6.5 80.9 %copy-start.3 = (s32[4]{0:T(128)S(1)}, s32[4]{0:T(128)}, u32[]{:S(2)}) copy-start(s32[4]{0:T(128)} %param.6) | copy-start | bytes 52
  15.1 87.5 %all-to-all-start = ((bf16[2,512,2048]{2,0,1:T(2,128)(2,1)}), bf16[2,512,2048]{2,0,1:T(2,128)(2,1)}, u32[]{:S(2)}, u32[]{:S(2)}) async-start(bf16[2,512,2048]{2,0,1:T(2,128)(2,1)} %bitcast.137), calls=%async_computation | async-start | bytes 8388608 | tf_op jit(solution)/shard_map/all_to_all | solution.py:97
  19.9 215.4 %reduce-scatter.2.cloned.1.call-start = ((), (), s32[]{:S(2)}) async-start(), calls=%async_computation.3 | async-start | bytes 2359296 | tf_op jit(solution)/shard_map/reduce_scatter | solution.py:100
  161.2 3.0 copy-start.1
  161.2 3.0 copy-start.2
  161.2 3.1 copy-start
  164.0 141.5 %all-gather.2.cloned.1.call-start = ((), (), s32[]{:S(2)}) async-start(), calls=%async_computation.4 | async-start | bytes 1179648 | tf_op jit(solution)/shard_map/all_gather | solution.py:102
Sparse Core Ops, SparseCore 0:
  164.1 71.2 reduce-scatter.1
  237.6 39.2 all-gather.1
where the time goes:
time: 453 us; the launch traced here: 452 us
  other arithmetic  199 us (44%)
  waiting for transfers between devices  70.9 us (16%)
  local copies, waits for them, and re-layouts  57.8 us (13%)
  matrix products  53.2 us (12%)
  blocking collectives  51.9 us (11%)
  between operations  13.6 us (3%)
  starting transfers between devices  5.36 us (1%)
    another operation x4, other arithmetic  142 us
    reduce_scatter x1, waiting for transfers between devices, on_device(): lax.psum_scatter(contribution, 'facet', scatter_dimension=2, tiled=True)  70.9 us
    all_to_all x1, blocking collectives, on_device(): lax.all_to_all(update, 'strip', split_axis=2, concat_axis=1, tiled=True)  51.9 us
    dot_general x1, matrix products, adjoint(): jnp.einsum('mj,xpj->pmx', untwisted.reshape(-1, SG), kernel_table.reshape...  31.5 us
    reduce_sum x1, other arithmetic, adjoint(): jnp.sum(image_real * cos_phi - image_imag * sin_phi, axis=0) * scale  26.7 us
    dot_general x1, matrix products, forward(): jnp.dot(twisted.reshape(-1, rows), kernel_table, preferred_element_type=j...  21.8 us
    concatenate x1, other arithmetic, dft_kernel(): jnp.concatenate([jnp.cos(angle), jnp.sin(angle)], axis=1)  13.7 us
    another operation x1, local copies, waits for them, and re-layouts, adjoint(): return jnp.stack([total_real, total_imag])  11.1 us
  transfers between devices with their start and end apart: 3, of which 1 were waited for; matrix products, arithmetic and copies ran while one was open for 33% of the time, Pallas kernels for 0%

commit v1 on v0

--- a/solution.py
+++ b/solution.py
@@ -101,7 +101,10 @@
     residual = weigh(model, visibilities, weights, mask)
     gathered = lax.all_gather(residual, "facet", axis=2, tiled=True)
     update = adjoint(gathered, 0, facet_index, offsets, kernel_table).astype(jnp.bfloat16)
-    result = lax.all_to_all(update, "strip", split_axis=2, concat_axis=1, tiled=True)
+    result = jnp.concatenate(
+        lax.all_to_all(jnp.stack(jnp.split(update, lax.axis_size("strip"), axis=2)), "strip", 0, 0),
+        axis=1,
+    )
     return result[None]
 
 

time: 453 us -> 431 us (0.951)
  local copies, waits for them, and re-layouts: 57.8 us -> 41.1 us
    another operation x1 -> x0, local copies, waits for them, and re-layouts: 11.1 us -> none  [adjoint(): return jnp.stack([total_real, total_imag])]
    all_to_all x2 -> x1, local copies, waits for them, and re-layouts: 8.68 us -> 2.32 us  [on_device(): lax.all_to_all(jnp.stack(jnp.split(update, lax.axis_size('strip'), axis=2...]
    another operation x5 -> x6, other arithmetic: 145 us -> 143 us
    unnamed x10 -> x12, local copies, waits for them, and re-layouts: 8.67 us -> 9.38 us
  transfers between devices with their start and end apart: 3 -> 3, of which waited for: 1 -> 1; matrix products, arithmetic and copies ran while one was open for 33% -> 35% of each run, Pallas kernels for 0% -> 0%
where the time goes in v1:
time: 431 us; the launch traced here: 430 us
  other arithmetic  195 us (45%)
  waiting for transfers between devices  70.8 us (16%)
  matrix products  53.2 us (12%)
  blocking collectives  50.7 us (12%)
  local copies, waits for them, and re-layouts  41.1 us (10%)
  between operations  13.7 us (3%)
  starting transfers between devices  5.35 us (1%)
    another operation x4, other arithmetic  142 us
    reduce_scatter x1, waiting for transfers between devices, on_device(): lax.psum_scatter(contribution, 'facet', scatter_dimension=2, tiled=True)  70.8 us
    all_to_all x1, blocking collectives, on_device(): lax.all_to_all(jnp.stack(jnp.split(update, lax.axis_size('strip'), axis=2...  50.7 us
    dot_general x1, matrix products, adjoint(): jnp.einsum('mj,xpj->pmx', untwisted.reshape(-1, SG), kernel_table.reshape...  31.5 us
    reduce_sum x1, other arithmetic, adjoint(): jnp.sum(image_real * cos_phi - image_imag * sin_phi, axis=0) * scale  26.7 us
    dot_general x1, matrix products, forward(): jnp.dot(twisted.reshape(-1, rows), kernel_table, preferred_element_type=j...  21.8 us
    concatenate x1, other arithmetic, dft_kernel(): jnp.concatenate([jnp.cos(angle), jnp.sin(angle)], axis=1)  13.7 us
    convert_element_type x2, local copies, waits for them, and re-layouts, forward(): real_part = data[0].astype(jnp.float32)[None]  11 us
  transfers between devices with their start and end apart: 3, of which 1 were waited for; matrix products, arithmetic and copies ran while one was open for 35% of the time, Pallas kernels for 0%

profile of v1, /device:TPU:0, one launch (start us, length us, event | category | flops | bytes accessed | tf_op | source)
XLA Modules:
  0.0 430.1 jit_solution(9793509027000645802)
XLA Ops:
  6.5 8.5 %copy.97 = bf16[1,2,512,2048]{3,1,2,0:T(2,128)(2,1)} copy(bf16[1,2,512,2048]{3,2,1,0:T(8,128)(2,1)} %param.5) | data formatting | bytes 8388608 | tf_op args[0]
  15.0 4.9 %all-to-all-start = ((bf16[2,512,2048]{2,0,1:T(2,128)(2,1)}), bf16[2,512,2048]{2,0,1:T(2,128)(2,1)}, u32[]{:S(2)}, u32[]{:S(2)}) async-start(bf16[2,512,2048]{2,0,1:T(2,128)(2,1)} %bitcast.126), calls=%async_computation | async-start | bytes 8388608 | tf_op jit(solution)/shard_map/all_to_all | solution.py:97
  19.9 0.2 reduce-scatter.2.cloned.1.call-start
  20.2 67.2 %sine_convert_fusion = (bf16[8192,512]{0,1:T(8,128)(2,1)}, bf16[8192,512]{0,1:T(8,128)(2,1)}) fusion(), kind=kLoop, calls=%fused_computation.29 | loop fusion | flops 67108864 | bytes 16777216 | tf_op jit(solution)/shard_map/convert.11
  87.6 13.7 %pad_maximum_fusion = bf16[8192,1024]{0,1:T(8,128)(2,1)} fusion(bf16[8192,512]{0,1:T(8,128)(2,1)} %get-tuple-element.23, bf16[8192,512]{0,1:T(8,128)(2,1)} %get-tuple-element.24), kind=kLoop, calls=%fused_computation.26 | loop fusion | flops 33554432 | bytes 33554432 | tf_op jit(solution)/shard_map/concatenate | solution.py:22
  101.3 1.2 fusion.38
  102.5 4.1 copy.75
  106.6 4.4 %slice_convert_fusion.1 = (f32[1,128,4,2048]{3,1,2,0:T(8,128)}, f32[1,128,4,2048]{3,1,2,0:T(8,128)}) fusion(bf16[2,128,4,2048]{3,1,2,0:T(8,128)(2,1)S(1)} %bitcast.124), kind=kLoop, calls=%fused_computation.54 | loop fusion | flops 2097152 | bytes 12582912 | tf_op jit(solution)/shard_map/convert_element_type | solution.py:42
  111.0 5.4 %copy.76 = f32[1,128,4,2048]{1,3,2,0:T(8,128)} copy(f32[1,128,4,2048]{3,1,2,0:T(8,128)} %get-tuple-element.15) | data formatting | bytes 8388608 | tf_op jit(solution)/shard_map/convert_element_type | solution.py:42
  116.3 5.7 %copy.77 = f32[128,8192]{1,0:T(8,128)} copy(f32[128,8192]{0,1:T(8,128)} %bitcast.127) | data formatting | bytes 8388608 | tf_op jit(solution)/shard_map/convert_element_type | solution.py:42
  122.0 5.3 %copy.78 = f32[1,128,4,2048]{1,3,2,0:T(8,128)} copy(f32[1,128,4,2048]{3,1,2,0:T(8,128)} %get-tuple-element.16) | data formatting | bytes 8388608 | tf_op jit(solution)/shard_map/convert_element_type | solution.py:43
  127.3 5.6 %copy.79 = f32[128,8192]{1,0:T(8,128)} copy(f32[128,8192]{0,1:T(8,128)} %bitcast.128) | data formatting | bytes 8388608 | tf_op jit(solution)/shard_map/convert_element_type | solution.py:43
  133.0 6.5 %add_convert_fusion = (bf16[4,1,128,8192]{3,2,1,0:T(8,128)(2,1)S(1)}, bf16[4,1,128,8192]{3,2,1,0:T(8,128)(2,1)S(1)}) fusion(f32[4,8192]{1,0:T(4,128)S(1)} %get-tuple-element.22, f32[128,8192]{1,0:T(8,128)} %copy.79, f32[4,8192]{1,0:T(4,128)S(1)} %get-tuple-element.21, f32[128,8192]{1,0:T(8,128)} %copy.77), kind=kLoop, calls=%fused_computation.34 | loop fusion | flops 33554432 | bytes 25427968 | tf_op jit(solution)/shard_map/convert.12
  139.5 21.8 %fusion.13 = f32[4,2,128,2,512]{4,2,3,1,0:T(8,128)S(1)} fusion(bf16[2,512,8192,1,1]{2,1,0,4,3:T(8,128)(2,1)} %bitcast.125, bf16[4,1,128,8192]{3,2,1,0:T(8,128)(2,1)S(1)} %get-tuple-element.8, bf16[4,1,128,8192]{3,2,1,0:T(8,128)(2,1)S(1)} %get-tuple-element.7), kind=kOutput, calls=%fused_computation.23 | convolution fusion | flops 17213423616 | bytes 37748736 | tf_op jit(solution)/shard_map/dot_general | solution.py:48
  161.3 0.7 add_multiply_fusion
  162.0 0.2 maximum_bitcast_fusion.2
  162.2 1.8 copy.82
  164.0 0.3 all-gather.2.cloned.1.call-start
  164.6 70.8 %reduce-scatter.2.cloned.1.call-done = f32[2,128,256]{1,2,0:T(8,128)} async-done(((f32[2,128,2048]{1,2,0:T(8,128)}), f32[2,128,256]{1,2,0:T(8,128)}) %reduce-scatter.2.cloned.1.call-update) | async-done | bytes 262160 | tf_op jit(solution)/shard_map/reduce_scatter | solution.py:100
  235.4 1.6 multiply_convert_fusion.2
  237.0 68.3 %sine_convert_fusion.1 = (bf16[8192,1,512]{2,0,1:T(8,128)(2,1)}, bf16[8192,1,512]{2,0,1:T(8,128)(2,1)}) fusion(), kind=kLoop, calls=%fused_computation.35 | loop fusion | flops 67108864 | bytes 16777216 | tf_op jit(solution)/shard_map/convert.15
  305.4 1.5 copy.84
  306.9 0.3 subtract_convert_fusion.1
  307.3 31.5 %fusion.9 = f32[8192,2,1024]{0,2,1:T(8,128)} fusion(bf16[1024,512,1]{1,0,2:T(8,128)(2,1)S(1)} %bitcast.132, bf16[8192,1,512]{2,0,1:T(8,128)(2,1)} %get-tuple-element.25, bf16[8192,1,512]{2,0,1:T(8,128)(2,1)} %get-tuple-element.26), kind=kOutput, calls=%fused_computation.18 | convolution fusion | flops 17188257792 | bytes 84934656 | tf_op jit(solution)/shard_map/mj,xpj->pmx/dot_general | solution.py:72
  338.8 26.7 %subtract_reduce_fusion = (f32[128,8192]{1,0:T(8,128)}, f32[128,8192]{1,0:T(8,128)}) fusion(f32[4,8192]{1,0:T(4,128)S(1)} %get-tuple-element.22, f32[4,8192]{1,0:T(4,128)S(1)} %get-tuple-element.21, f32[2,4,2,128,8192]{4,3,2,1,0:T(8,128)} %bitcast.25), kind=kLoop, calls=%fused_computation.28 | loop fusion | flops 39845888 | bytes 75759616 | tf_op jit(solution)/shard_map/reduce_sum | solution.py:85
  365.4 2.7 fusion.22
  368.2 0.7 copy-done
  368.9 0.4 fusion.23
  369.3 0.3 fusion.27
  369.6 0.6 pad_maximum_fusion.1
  370.2 50.7 %all_to_all.20 = bf16[4,2,128,2048]{3,2,1,0:T(8,128)(2,1)S(1)} all-to-all(bf16[4,2,128,2048]{3,2,1,0:T(8,128)(2,1)S(1)} %pad_maximum_fusion.1), channel_id=1, replica_groups=mesh['facet'=8,'strip'=4] {'strip'}, dimensions={0} | all-to-all | bytes 8388608 | tf_op jit(solution)/shard_map/all_to_all | solution.py:105
  420.9 2.3 copy.89
  (20 shorter events, 0.6 us)
Async XLA Ops:
  15.0 87.5 %all-to-all-start = ((bf16[2,512,2048]{2,0,1:T(2,128)(2,1)}), bf16[2,512,2048]{2,0,1:T(2,128)(2,1)}, u32[]{:S(2)}, u32[]{:S(2)}) async-start(bf16[2,512,2048]{2,0,1:T(2,128)(2,1)} %bitcast.126), calls=%async_computation | async-start | bytes 8388608 | tf_op jit(solution)/shard_map/all_to_all | solution.py:97
  19.9 215.5 %reduce-scatter.2.cloned.1.call-start = ((), (), s32[]{:S(2)}) async-start(), calls=%async_computation.3 | async-start | bytes 2359296 | tf_op jit(solution)/shard_map/reduce_scatter | solution.py:100
  20.2 67.2 %copy-start.4 = (s32[4]{0:T(128)S(1)}, s32[4]{0:T(128)}, u32[]{:S(2)}) copy-start(s32[4]{0:T(128)} %param.6) | copy-start | bytes 52
  161.3 3.0 copy-start.2
  161.3 3.0 copy-start.3
  161.3 3.1 copy-start.1
  164.0 141.3 %all-gather.2.cloned.1.call-start = ((), (), s32[]{:S(2)}) async-start(), calls=%async_computation.4 | async-start | bytes 1179648 | tf_op jit(solution)/shard_map/all_gather | solution.py:102
  365.4 3.4 copy-start
Sparse Core Ops, SparseCore 0:
  164.2 71.1 reduce-scatter.1
  237.6 39.2 all-gather.1
